TPU v7x, 32 devices: a whole 2x2x4 slice. The times are simulated.
32 devices in a mesh: chain: 2 (over y), cell: 4 (over z), col: 4 (over x, core).
Axes of the slice: x: 2, y: 2, z: 4, core: 2. Of those that a mesh axis runs over, the one named last changes fastest.
Arguments:
- grad: float32 [16384, 64], P(('chain', 'cell', 'col')), parts along dimension 0, may hold values from -6 to 6
- near_tiles: bfloat16 [4, 2, 2048, 2048], P('cell', None, 'col'), may hold values from -0.09375 to 0.09375
- tile_count: int32 [4], replicated, may hold values from 1 to 2
- near_offset: int32 [4], replicated, may hold values from -2 to 2, as said below
- far_src: int32 [4, 8], replicated, may hold values from 0 to 3
- far_count: int32 [4], replicated, may hold values from 1 to 8
- far_cores: float32 [4, 8, 64, 64], P('cell'), may hold values from -0.25 to 0.25
- basis_out: bfloat16 [8192, 64], P(('cell', 'col')), may hold values from -0.75 to 0.75
- basis_in: bfloat16 [8192, 64], P(('cell', 'col')), may hold values from -0.125 to 0.125
Outputs:
- step_block: float32 [16384, 64], P(('chain', 'cell', 'col')), parts along dimension 0
There are 2 independent parts, one for each index of `chain`. A program takes and returns all parts, laid end to end along the dimension named above; an argument that names none is the same for every part. Nothing has to cross between parts.
Inputs may be any that keep to these rules, and one draw needn't show every extreme that they name: c + near_offset[c] is a cluster of the chain, and near_offset[c] is never 0.
All inputs are finite; a program needn't handle non-finite values.
Results may differ from a plain program's by a relative error of at most 0.0035.
Values may be sent and summed in bfloat16 or wider, within the bound.
No kernel may reach another device: no remote copies, remote signals or barrier semaphores. Data moves between devices by JAX's collectives and lax.ppermute only.
A program may use at most 64 MiB of HBM per device.

v0:
```python
import jax
import jax.numpy as jnp
from jax import lax
from jax.sharding import PartitionSpec as P


def shifted(value, axis, by):
    devices = lax.axis_size(axis)
    pairs = [(i, i + by) for i in range(devices) if 0 <= i + by < devices]
    return lax.ppermute(value, axis, pairs)


def pick_offset(stacked, offset):
    position = offset + 2 - (offset > 0).astype(jnp.int32)
    return lax.dynamic_index_in_dim(stacked, position, 0, keepdims=False)


def coupling(table, sources, count, cores):
    picked = jnp.take(table, sources, axis=0)
    slots = jnp.arange(cores.shape[0], dtype=jnp.int32)
    masked = jnp.where((slots < count)[:, None, None], cores, jnp.zeros_like(cores))
    return jnp.einsum("kab,kbw->aw", masked, picked, precision=lax.Precision.HIGHEST)


def body(
    grad, near_tiles, tile_count, near_offset, far_src, far_count, far_cores, basis_out, basis_in
):
    owner = lax.axis_index("cell")
    rounded = grad.astype(jnp.bfloat16)
    offset = near_offset[owner]
    steps_list = (-2, -1, 1, 2)
    whole = lax.all_gather(rounded, "col", axis=0, tiled=True)
    moved = [shifted(whole, "cell", -step) for step in steps_list]
    beside = pick_offset(jnp.stack(moved), offset)
    tiles = near_tiles[0]
    own_term = jnp.dot(tiles[0], whole, preferred_element_type=jnp.float32)
    other_term = jnp.dot(tiles[1], beside, preferred_element_type=jnp.float32)
    near = own_term + jnp.where(tile_count[owner] == 2, other_term, jnp.zeros_like(other_term))
    partial_proj = lax.dot_general(
        basis_in, rounded, (((0,), (0,)), ((), ())), preferred_element_type=jnp.float32
    )
    sources = far_src[owner]
    count = far_count[owner]
    cores = far_cores[0]
    proj = lax.psum(partial_proj, "col")
    table = lax.all_gather(proj[None], "cell", axis=0, tiled=True)
    core_block = coupling(table, sources, count, cores).astype(jnp.bfloat16)
    far = jnp.dot(basis_out, core_block, preferred_element_type=jnp.float32)
    return near + far


def solution(mesh):
    placed = (
        P(("chain", "cell", "col"), None),
        P("cell", None, "col", None),
        P(),
        P(),
        P(),
        P(),
        P("cell", None, None, None),
        P(("cell", "col"), None),
        P(("cell", "col"), None),
    )
    return jax.shard_map(
        body,
        mesh=mesh,
        in_specs=placed,
        out_specs=P(("chain", "cell", "col"), None),
        check_vma=False,
    )
```

profile of v0, /device:TPU:0, one launch (start us, length us, event | category | flops | bytes accessed | tf_op | source)
XLA Modules:
  0.0 60.8 jit_solution(2780922674257491303)
XLA Ops:
  0.0 0.0 copy-start
  0.0 0.9 %convert_element_type.10 = bf16[512,64]{0,1:T(8,128)(2,1)S(1)} convert(f32[512,64]{0,1:T(8,128)} %param.9) | non-fusion elementwise | flops 32768 | bytes 196608 | tf_op jit(solution)/shard_map/convert_element_type | solution.py:29
  1.0 7.2 %all_gather.6 = bf16[2048,64]{0,1:T(8,128)(2,1)S(1)} all-gather(bf16[512,64]{0,1:T(8,128)(2,1)S(1)} %convert_element_type.10), channel_id=1, replica_groups=mesh['chain'=2,'cell'=4,'col'=4] {'col'}, dimensions={0}, use_global_device_ids=true | all-gather | bytes 327680 | tf_op jit(solution)/shard_map/all_gather | solution.py:32
  8.2 4.5 %collective-permute-start = (bf16[2048,64]{0,1:T(8,128)(2,1)S(1)}, bf16[2048,64]{0,1:T(8,128)(2,1)S(1)}, u32[]{:S(2)}, u32[]{:S(2)}) collective-permute-start(bf16[2048,64]{0,1:T(8,128)(2,1)S(1)} %all_gather.6), channel_id=1, source_target_pairs={{0,8},{4,12},{1,9},{5,13},{2,10},{6,14},{3,11},{7,15},{16,24},{20,... | collective-permute-start | bytes 786440 | tf_op jit(solution)/shard_map/ppermute | solution.py:10
  12.7 3.5 %collective-permute-start.1 = (bf16[2048,64]{0,1:T(8,128)(2,1)S(1)}, bf16[2048,64]{0,1:T(8,128)(2,1)S(1)}, u32[]{:S(2)}, u32[]{:S(2)}) collective-permute-start(bf16[2048,64]{0,1:T(8,128)(2,1)S(1)} %all_gather.6), channel_id=1, source_target_pairs={{0,4},{4,8},{8,12},{1,5},{5,9},{9,13},{2,6},{6,10},{10,14},{3,7},{... | collective-permute-start | bytes 786440 | tf_op jit(solution)/shard_map/ppermute | solution.py:10
  16.2 1.3 %collective-permute-start.2 = (bf16[2048,64]{0,1:T(8,128)(2,1)S(1)}, bf16[2048,64]{0,1:T(8,128)(2,1)S(1)}, u32[]{:S(2)}, u32[]{:S(2)}) collective-permute-start(bf16[2048,64]{0,1:T(8,128)(2,1)S(1)} %all_gather.6), channel_id=1, source_target_pairs={{4,0},{8,4},{12,8},{5,1},{9,5},{13,9},{6,2},{10,6},{14,10},{7,3},{... | collective-permute-start | bytes 786440 | tf_op jit(solution)/shard_map/ppermute | solution.py:10
  17.5 1.3 %collective-permute-start.3 = (bf16[2048,64]{0,1:T(8,128)(2,1)S(1)}, bf16[2048,64]{0,1:T(8,128)(2,1)S(1)}, u32[]{:S(2)}, u32[]{:S(2)}) collective-permute-start(bf16[2048,64]{0,1:T(8,128)(2,1)S(1)} %all_gather.6), channel_id=1, source_target_pairs={{8,0},{12,4},{9,1},{13,5},{10,2},{14,6},{11,3},{15,7},{24,16},{28,... | collective-permute-start | bytes 786440 | tf_op jit(solution)/shard_map/ppermute | solution.py:10
  18.8 1.2 %dynamic_slice.19 = s32[1]{0:T(128)} dynamic-slice(s32[4]{0:T(128)} %param.14, s32[]{:T(128)S(6)} %select_n.45), dynamic_slice_sizes={1} | dynamic-slice | bytes 12 | tf_op jit(solution)/shard_map/dynamic_slice | solution.py:43
  20.1 0.7 %fusion.30 = s32[8]{0:T(128)S(1)} fusion(s32[4,8]{1,0:T(4,128)} %param.13, s32[]{:T(128)S(6)} %select_n.45), kind=kLoop, calls=%fused_computation.35 | loop fusion | flops 24 | bytes 68 | tf_op jit(solution)/shard_map/jit(_take)/jit(_where)/select_n | solution.py:19
  20.8 1.3 %compare_and_fusion = (pred[8]{0:T(512)(128)(4,1)S(1)}, pred[8]{0:T(512)(128)(4,1)S(1)}) fusion(s32[4,8]{1,0:T(4,128)} %param.13, s32[]{:T(128)S(6)} %select_n.45, s32[]{:T(128)} %bitcast.10), kind=kLoop, calls=%fused_computation.32 | loop fusion | flops 56 | bytes 56 | tf_op jit(solution)/shard_map/jit(_take)/and | solution.py:19
  22.1 1.0 %convolution_bitcast_fusion.1 = f32[1,64,64]{2,1,0:T(8,128)S(1)} fusion(bf16[512,64]{0,1:T(8,128)(2,1)} %param.17, bf16[512,64]{0,1:T(8,128)(2,1)S(1)} %convert_element_type.10), kind=kOutput, calls=%fused_computation.12 | convolution fusion | flops 4194304 | bytes 147456 | tf_op jit(solution)/shard_map/dot_general | solution.py:39
  23.1 11.4 %psum.7 = f32[1,64,64]{2,1,0:T(8,128)S(1)} all-reduce(f32[1,64,64]{2,1,0:T(8,128)S(1)} %convolution_bitcast_fusion.1), channel_id=1, replica_groups=mesh['chain'=2,'cell'=4,'col'=4] {'col'}, use_global_device_ids=true, to_apply=%region_0.1 | all-reduce | flops 4096 | bytes 32768 | tf_op jit(solution)/shard_map/psum | solution.py:45
  34.5 14.3 %all_gather.7 = f32[4,64,64]{2,1,0:T(8,128)S(1)} all-gather(f32[1,64,64]{2,1,0:T(8,128)S(1)} %psum.7), channel_id=1, replica_groups=mesh['chain'=2,'cell'=4,'col'=4] {'cell'}, dimensions={0}, use_global_device_ids=true | all-gather | bytes 81920 | tf_op jit(solution)/shard_map/all_gather | solution.py:46
  48.8 0.6 gather_fusion
  49.3 1.4 %fusion.18 = bf16[64,64]{1,0:T(8,128)(2,1)S(1)} fusion(f32[1,8,64,64]{3,2,1,0:T(8,128)} %param.15, f32[8,64,64]{2,1,0:T(8,128)S(1)} %gather_fusion, pred[8]{0:T(512)(128)(4,1)S(1)} %get-tuple-element.5, pred[8]{0:T(512)(128)(4,1)S(1)} %get-tuple-element.6), kind=kOutput, calls=%fused_computation.14 | convolution fusion | flops 25235456 | bytes 270352 | tf_op jit(solution)/shard_map/kab,kbw->aw/dot_general | solution.py:22
  50.8 1.2 %dynamic_slice.17 = s32[1]{0:T(128)} dynamic-slice(s32[4]{0:T(128)} %param.12, s32[]{:T(128)S(6)} %select_n.45), dynamic_slice_sizes={1} | dynamic-slice | bytes 12 | tf_op jit(solution)/shard_map/dynamic_slice | solution.py:30
  53.3 1.3 %dynamic_slice.16 = s32[1]{0:T(128)} dynamic-slice(s32[4]{0:T(128)} %param.11, s32[]{:T(128)S(6)} %select_n.45), dynamic_slice_sizes={1} | dynamic-slice | bytes 12 | tf_op jit(solution)/shard_map/dynamic_slice | solution.py:38
  55.2 0.2 convolution_bitcast_fusion
  55.4 0.0 collective-permute-done
  55.4 0.0 collective-permute-done.1
  55.4 0.0 collective-permute-done.2
  55.4 0.0 collective-permute-done.3
  55.4 2.4 %fusion.15 = f32[512,64]{0,1:T(8,128)S(1)} fusion(bf16[1,2,512,2048]{3,2,1,0:T(8,128)(2,1)} %param.10, s32[]{:T(128)S(6)} %select_n.47, bf16[1,2048,64]{1,2,0:T(8,128)(2,1)S(1)} %bitcast.48, bf16[1,2048,64]{1,2,0:T(8,128)(2,1)S(1)} %bitcast.49, bf16[1,2048,64]{1,2,0:T(8,128)(2,1)S(1)} %bitcast.50, bf16[1,2048,64]{1,2,0:T(8,128)(2,1)S(1)} %bitcast.51, ...), kind=kOutput, calls=%fused_computation.10 | convolution fusion | flops 134643712 | bytes 3277316 | tf_op jit(solution)/shard_map/dot_general | solution.py:37
  57.8 3.0 %fusion.9 = f32[512,64]{0,1:T(8,128)} fusion(f32[512,64]{0,1:T(8,128)S(1)} %convolution_bitcast_fusion, f32[512,64]{0,1:T(8,128)S(1)} %fusion.15, bf16[2048,64]{0,1:T(8,128)(2,1)S(1)} %all_gather.6, bf16[1,2,512,2048]{3,2,1,0:T(8,128)(2,1)} %param.10), kind=kOutput, calls=%fused_computation.8 | convolution fusion | flops 134283264 | bytes 2752512 | tf_op jit(solution)/shard_map/dot_general | solution.py:36
  (2 shorter events, 0.0 us)
Async XLA Ops:
  0.0 55.2 %copy-start = (bf16[512,64]{0,1:T(8,128)(2,1)S(1)}, bf16[512,64]{0,1:T(8,128)(2,1)}, u32[]{:S(2)}) copy-start(bf16[512,64]{0,1:T(8,128)(2,1)} %param.16) | copy-start | bytes 196612
  8.2 47.2 %collective-permute-start = (bf16[2048,64]{0,1:T(8,128)(2,1)S(1)}, bf16[2048,64]{0,1:T(8,128)(2,1)S(1)}, u32[]{:S(2)}, u32[]{:S(2)}) collective-permute-start(bf16[2048,64]{0,1:T(8,128)(2,1)S(1)} %all_gather.6), channel_id=1, source_target_pairs={{0,8},{4,12},{1,9},{5,13},{2,10},{6,14},{3,11},{7,15},{16,24},{20,... | collective-permute-start | bytes 786440 | tf_op jit(solution)/shard_map/ppermute | solution.py:10
  12.7 42.7 %collective-permute-start.1 = (bf16[2048,64]{0,1:T(8,128)(2,1)S(1)}, bf16[2048,64]{0,1:T(8,128)(2,1)S(1)}, u32[]{:S(2)}, u32[]{:S(2)}) collective-permute-start(bf16[2048,64]{0,1:T(8,128)(2,1)S(1)} %all_gather.6), channel_id=1, source_target_pairs={{0,4},{4,8},{8,12},{1,5},{5,9},{9,13},{2,6},{6,10},{10,14},{3,7},{... | collective-permute-start | bytes 786440 | tf_op jit(solution)/shard_map/ppermute | solution.py:10
  16.2 39.2 %collective-permute-start.2 = (bf16[2048,64]{0,1:T(8,128)(2,1)S(1)}, bf16[2048,64]{0,1:T(8,128)(2,1)S(1)}, u32[]{:S(2)}, u32[]{:S(2)}) collective-permute-start(bf16[2048,64]{0,1:T(8,128)(2,1)S(1)} %all_gather.6), channel_id=1, source_target_pairs={{4,0},{8,4},{12,8},{5,1},{9,5},{13,9},{6,2},{10,6},{14,10},{7,3},{... | collective-permute-start | bytes 786440 | tf_op jit(solution)/shard_map/ppermute | solution.py:10
  17.5 37.9 %collective-permute-start.3 = (bf16[2048,64]{0,1:T(8,128)(2,1)S(1)}, bf16[2048,64]{0,1:T(8,128)(2,1)S(1)}, u32[]{:S(2)}, u32[]{:S(2)}) collective-permute-start(bf16[2048,64]{0,1:T(8,128)(2,1)S(1)} %all_gather.6), channel_id=1, source_target_pairs={{8,0},{12,4},{9,1},{13,5},{10,2},{14,6},{11,3},{15,7},{24,16},{28,... | collective-permute-start | bytes 786440 | tf_op jit(solution)/shard_map/ppermute | solution.py:10
where the time goes:
time: 61.3 us; the launch traced here: 60.8 us
  blocking collectives  32.9 us (54%)
  starting transfers between devices  10.6 us (17%)
  matrix products  7.95 us (13%)
  local copies, waits for them, and re-layouts  4.33 us (7%)
  other arithmetic  2.98 us (5%)
  between operations  2.04 us (3%)
    all_gather x1, blocking collectives, body(): table = lax.all_gather(proj[None], 'cell', axis=0, tiled=True)  14.3 us
    psum x1, blocking collectives, body(): proj = lax.psum(partial_proj, 'col')  11.4 us
    ppermute x4, starting transfers between devices, shifted(): return lax.ppermute(value, axis, pairs)  10.6 us
    all_gather x1, blocking collectives, body(): whole = lax.all_gather(rounded, 'col', axis=0, tiled=True)  7.22 us
    dot_general x1, matrix products, body(): own_term = jnp.dot(tiles[0], whole, preferred_element_type=jnp.float32)  3.01 us
    dot_general x1, matrix products, body(): other_term = jnp.dot(tiles[1], beside, preferred_element_type=jnp.float32)  2.36 us
    dot_general x1, matrix products, coupling(): jnp.einsum('kab,kbw->aw', masked, picked, precision=lax.Precision.HIGHEST)  1.42 us
    and x1, other arithmetic, coupling(): picked = jnp.take(table, sources, axis=0)  1.34 us
  transfers between devices with their start and end apart: 4, of which 0 were waited for; matrix products, arithmetic and copies ran while one was open for 15% of the time, Pallas kernels for 0%

commit v1 on v0

--- a/solution.py
+++ b/solution.py
@@ -2,6 +2,12 @@
 import jax.numpy as jnp
 from jax import lax
 from jax.sharding import PartitionSpec as P
+
+
+def in_order(parts, dim):
+    shape = list(parts.shape[1:])
+    shape[dim] *= parts.shape[0]
+    return jnp.moveaxis(parts, 0, dim).reshape(shape)
 
 
 def shifted(value, axis, by):
@@ -29,7 +35,19 @@
     rounded = grad.astype(jnp.bfloat16)
     offset = near_offset[owner]
     steps_list = (-2, -1, 1, 2)
-    whole = lax.all_gather(rounded, "col", axis=0, tiled=True)
+    devices_2 = lax.axis_size("col")
+    pairs_2 = [(i_2, (i_2 + 1) % devices_2) for i_2 in range(devices_2)]
+    back = [(b, a) for a, b in pairs_2]
+    lower, upper = ([], [])
+    for k in range(devices_2 - 1):
+        if k % 2 == 0:
+            lower.append(lax.ppermute(lower[-1] if lower else rounded, "col", pairs_2))
+        else:
+            upper.append(lax.ppermute(upper[-1] if upper else rounded, "col", back))
+    blocks = jnp.stack([*lower[::-1], rounded, *upper])
+    shift = lax.axis_index("col") - len(lower)
+    blocks = blocks[(jnp.arange(devices_2) - shift) % devices_2]
+    whole = in_order(blocks, 0)
     moved = [shifted(whole, "cell", -step) for step in steps_list]
     beside = pick_offset(jnp.stack(moved), offset)
     tiles = near_tiles[0]

time: 61.3 us -> 65.2 us (1.064); the launches traced: 60.8 us -> 64 us
  blocking collectives: 32.9 us -> 24.6 us
  waiting for transfers between devices: 0.01 us -> 6.15 us
  starting transfers between devices: 10.6 us -> 14.2 us
  other arithmetic: 2.98 us -> 3.95 us
    all_gather x1 -> x0, blocking collectives: 7.22 us -> none  [body(): whole = lax.all_gather(rounded, 'col', axis=0, tiled=True)]
    ppermute x4, waiting for transfers between devices: 0.01 us -> 3.81 us  [shifted(): return lax.ppermute(value, axis, pairs)]
    ppermute x0 -> x3, starting transfers between devices: none -> 2.58 us  [the longest x1 1.98 us: body(): upper.append(lax.ppermute(upper[-1] if upper else rounded, 'col', back))]
    ppermute x0 -> x3, waiting for transfers between devices: none -> 2.34 us  [the longest x2 2.33 us: body(): lower.append(lax.ppermute(lower[-1] if lower else rounded, 'col', pairs_2))]
    ppermute x4, starting transfers between devices: 10.6 us -> 11.6 us  [shifted(): return lax.ppermute(value, axis, pairs)]
    another operation x0 -> x2, other arithmetic: none -> 0.95 us  [body(): blocks = jnp.stack([*lower[::-1], rounded, *upper])]
  transfers between devices with their start and end apart: 4 -> 7, of which waited for: 0 -> 2; matrix products, arithmetic and copies ran while one was open for 15% -> 15% of each run, Pallas kernels for 0% -> 0%
where the time goes in v1:
time: 65.2 us; the launch traced here: 64 us
  blocking collectives  24.6 us (38%)
  starting transfers between devices  14.2 us (22%)
  matrix products  7.94 us (12%)
  waiting for transfers between devices  6.15 us (9%)
  local copies, waits for them, and re-layouts  4.96 us (8%)
  other arithmetic  3.95 us (6%)
  between operations  2.17 us (3%)
    all_gather x1, blocking collectives, body(): table = lax.all_gather(proj[None], 'cell', axis=0, tiled=True)  13.8 us
    ppermute x4, starting transfers between devices, shifted(): return lax.ppermute(value, axis, pairs)  11.6 us
    psum x1, blocking collectives, body(): proj = lax.psum(partial_proj, 'col')  10.8 us
    ppermute x4, waiting for transfers between devices, shifted(): return lax.ppermute(value, axis, pairs)  3.81 us
    dot_general x1, matrix products, body(): own_term = jnp.dot(tiles[0], whole, preferred_element_type=jnp.float32)  3.02 us
    dot_general x1, matrix products, body(): other_term = jnp.dot(tiles[1], beside, preferred_element_type=jnp.float32)  2.35 us
    ppermute x2, waiting for transfers between devices, body(): lower.append(lax.ppermute(lower[-1] if lower else rounded, 'col', pairs_2))  2.33 us
    ppermute x1, starting transfers between devices, body(): upper.append(lax.ppermute(upper[-1] if upper else rounded, 'col', back))  1.98 us
  transfers between devices with their start and end apart: 7, of which 2 were waited for; matrix products, arithmetic and copies ran while one was open for 15% of the time, Pallas kernels for 0%

profile of v1, /device:TPU:0, one launch (start us, length us, event | category | flops | bytes accessed | tf_op | source)
XLA Modules:
  0.0 64.0 jit_solution(10837949486279774720)
XLA Ops:
  0.0 0.9 %convert_element_type.10 = bf16[512,64]{0,1:T(8,128)(2,1)S(1)} convert(f32[512,64]{0,1:T(8,128)} %param.9) | non-fusion elementwise | flops 32768 | bytes 196608 | tf_op jit(solution)/shard_map/convert_element_type | solution.py:35
  1.0 0.5 collective-permute-start
  1.5 2.0 %collective-permute-start.2 = (bf16[512,64]{0,1:T(8,128)(2,1)S(1)}, bf16[512,64]{0,1:T(8,128)(2,1)S(1)}, u32[]{:S(2)}, u32[]{:S(2)}) collective-permute-start(bf16[512,64]{0,1:T(8,128)(2,1)S(1)} %convert_element_type.10), channel_id=1, source_target_pairs={{1,0},{2,1},{3,2},{0,3},{5,4},{6,5},{7,6},{4,7},{9,8},{10,9},{11,1... | collective-permute-start | bytes 196616 | tf_op jit(solution)/shard_map/ppermute | solution.py:46
  3.5 0.9 %convert_bitcast_fusion = bf16[1,512,64]{1,2,0:T(8,128)(2,1)S(1)} fusion(f32[512,64]{0,1:T(8,128)} %param.9), kind=kLoop, calls=%fused_computation.49 | loop fusion | flops 32768 | bytes 196608 | tf_op jit(solution)/shard_map/stack | solution.py:47
  4.4 1.2 %dynamic_slice.19 = s32[1]{0:T(128)} dynamic-slice(s32[4]{0:T(128)} %param.14, s32[]{:T(128)S(6)} %select_n.69), dynamic_slice_sizes={1} | dynamic-slice | bytes 12 | tf_op jit(solution)/shard_map/dynamic_slice | solution.py:61
  5.7 0.7 %fusion.32 = s32[8]{0:T(128)S(1)} fusion(s32[4,8]{1,0:T(4,128)} %param.13, s32[]{:T(128)S(6)} %select_n.69), kind=kLoop, calls=%fused_computation.43 | loop fusion | flops 24 | bytes 68 | tf_op jit(solution)/shard_map/jit(_take)/jit(_where)/select_n | solution.py:25
  6.4 1.0 %convolution_bitcast_fusion = f32[1,64,64]{2,1,0:T(8,128)S(1)} fusion(bf16[512,64]{0,1:T(8,128)(2,1)} %param.17, bf16[512,64]{0,1:T(8,128)(2,1)S(1)} %convert_element_type.10), kind=kOutput, calls=%fused_computation.12 | convolution fusion | flops 4194304 | bytes 147456 | tf_op jit(solution)/shard_map/dot_general | solution.py:57
  7.3 10.8 %psum.7 = f32[1,64,64]{2,1,0:T(8,128)S(1)} all-reduce(f32[1,64,64]{2,1,0:T(8,128)S(1)} %convolution_bitcast_fusion), channel_id=1, replica_groups=mesh['chain'=2,'cell'=4,'col'=4] {'col'}, use_global_device_ids=true, to_apply=%region_0.1 | all-reduce | flops 4096 | bytes 32768 | tf_op jit(solution)/shard_map/psum | solution.py:63
  18.2 13.8 %all_gather.3 = f32[4,64,64]{2,1,0:T(8,128)S(1)} all-gather(f32[1,64,64]{2,1,0:T(8,128)S(1)} %psum.7), channel_id=1, replica_groups=mesh['chain'=2,'cell'=4,'col'=4] {'cell'}, dimensions={0}, use_global_device_ids=true | all-gather | bytes 81920 | tf_op jit(solution)/shard_map/all_gather | solution.py:64
  32.0 0.6 gather_fusion.1
  32.6 1.3 %compare_and_fusion = (pred[8]{0:T(512)(128)(4,1)S(1)}, pred[8]{0:T(512)(128)(4,1)S(1)}) fusion(s32[4,8]{1,0:T(4,128)} %param.13, s32[]{:T(128)S(6)} %select_n.69, s32[]{:T(128)} %bitcast.14), kind=kLoop, calls=%fused_computation.37 | loop fusion | flops 56 | bytes 56 | tf_op jit(solution)/shard_map/jit(_take)/and | solution.py:25
  34.0 2.3 %collective-permute-done.1 = bf16[512,64]{0,1:T(8,128)(2,1)S(1)} collective-permute-done((bf16[512,64]{0,1:T(8,128)(2,1)S(1)}, bf16[512,64]{0,1:T(8,128)(2,1)S(1)}, u32[]{:S(2)}, u32[]{:S(2)}) %collective-permute-start.1) | collective-permute-done | bytes 65568 | tf_op jit(solution)/shard_map/ppermute | solution.py:44
  36.3 0.6 gather_fusion
  36.9 1.3 %collective-permute-start.6 = (bf16[2048,64]{0,1:T(8,128)(2,1)S(1)}, bf16[2048,64]{0,1:T(8,128)(2,1)S(1)}, u32[]{:S(2)}, u32[]{:S(2)}) collective-permute-start(bf16[2048,64]{0,1:T(8,128)(2,1)S(1)} %bitcast.56), channel_id=1, source_target_pairs={{8,0},{12,4},{9,1},{13,5},{10,2},{14,6},{11,3},{15,7},{24,16},{28,... | collective-permute-start | bytes 786440 | tf_op jit(solution)/shard_map/ppermute | solution.py:16
  38.2 5.5 %collective-permute-start.3 = (bf16[2048,64]{0,1:T(8,128)(2,1)S(1)}, bf16[2048,64]{0,1:T(8,128)(2,1)S(1)}, u32[]{:S(2)}, u32[]{:S(2)}) collective-permute-start(bf16[2048,64]{0,1:T(8,128)(2,1)S(1)} %bitcast.57), channel_id=1, source_target_pairs={{0,8},{4,12},{1,9},{5,13},{2,10},{6,14},{3,11},{7,15},{16,24},{20,... | collective-permute-start | bytes 786440 | tf_op jit(solution)/shard_map/ppermute | solution.py:16
  43.7 3.5 %collective-permute-start.4 = (bf16[2048,64]{0,1:T(8,128)(2,1)S(1)}, bf16[2048,64]{0,1:T(8,128)(2,1)S(1)}, u32[]{:S(2)}, u32[]{:S(2)}) collective-permute-start(bf16[2048,64]{0,1:T(8,128)(2,1)S(1)} %bitcast.58), channel_id=1, source_target_pairs={{0,4},{4,8},{8,12},{1,5},{5,9},{9,13},{2,6},{6,10},{10,14},{3,7},{... | collective-permute-start | bytes 786440 | tf_op jit(solution)/shard_map/ppermute | solution.py:16
  47.3 1.3 %collective-permute-start.5 = (bf16[2048,64]{0,1:T(8,128)(2,1)S(1)}, bf16[2048,64]{0,1:T(8,128)(2,1)S(1)}, u32[]{:S(2)}, u32[]{:S(2)}) collective-permute-start(bf16[2048,64]{0,1:T(8,128)(2,1)S(1)} %bitcast.59), channel_id=1, source_target_pairs={{4,0},{8,4},{12,8},{5,1},{9,5},{13,9},{6,2},{10,6},{14,10},{7,3},{... | collective-permute-start | bytes 786440 | tf_op jit(solution)/shard_map/ppermute | solution.py:16
  48.6 1.4 %fusion.18 = bf16[64,64]{1,0:T(8,128)(2,1)S(1)} fusion(f32[1,8,64,64]{3,2,1,0:T(8,128)} %param.15, f32[8,64,64]{2,1,0:T(8,128)S(1)} %gather_fusion.1, pred[8]{0:T(512)(128)(4,1)S(1)} %get-tuple-element.5, pred[8]{0:T(512)(128)(4,1)S(1)} %get-tuple-element.6), kind=kOutput, calls=%fused_computation.14 | convolution fusion | flops 25235456 | bytes 270352 | tf_op jit(solution)/shard_map/kab,kbw->aw/dot_general | solution.py:28
  50.0 1.2 %dynamic_slice.17 = s32[1]{0:T(128)} dynamic-slice(s32[4]{0:T(128)} %param.12, s32[]{:T(128)S(6)} %select_n.69), dynamic_slice_sizes={1} | dynamic-slice | bytes 12 | tf_op jit(solution)/shard_map/dynamic_slice | solution.py:36
  52.5 1.3 %dynamic_slice.16 = s32[1]{0:T(128)} dynamic-slice(s32[4]{0:T(128)} %param.11, s32[]{:T(128)S(6)} %select_n.69), dynamic_slice_sizes={1} | dynamic-slice | bytes 12 | tf_op jit(solution)/shard_map/dynamic_slice | solution.py:56
  54.6 0.2 fusion.36
  54.8 3.8 %collective-permute-done.5 = bf16[2048,64]{0,1:T(8,128)(2,1)S(1)} collective-permute-done((bf16[2048,64]{0,1:T(8,128)(2,1)S(1)}, bf16[2048,64]{0,1:T(8,128)(2,1)S(1)}, u32[]{:S(2)}, u32[]{:S(2)}) %collective-permute-start.5) | collective-permute-done | bytes 262176 | tf_op jit(solution)/shard_map/ppermute | solution.py:16
  58.6 2.4 %fusion.15 = f32[64,512]{1,0:T(8,128)S(1)} fusion(bf16[1,2,512,2048]{3,2,1,0:T(8,128)(2,1)} %param.10, s32[]{:T(128)S(6)} %select_n.71, bf16[1,2048,64]{1,2,0:T(8,128)(2,1)S(1)} %bitcast.65, bf16[1,2048,64]{1,2,0:T(8,128)(2,1)S(1)} %bitcast.66, bf16[1,2048,64]{1,2,0:T(8,128)(2,1)S(1)} %bitcast.67, bf16[1,2048,64]{1,2,0:T(8,128)(2,1)S(1)} %bitcast.64, ...), kind=kOutput, calls=%fused_computation.11 | convolution fusion | flops 134643712 | bytes 3277316 | tf_op jit(solution)/shard_map/dot_general | solution.py:55
  60.9 3.0 %fusion.12 = f32[512,64]{0,1:T(8,128)} fusion(f32[64,512]{1,0:T(8,128)S(1)} %fusion.36, f32[64,512]{1,0:T(8,128)S(1)} %fusion.15, bf16[2048,64]{0,1:T(8,128)(2,1)S(1)} %bitcast.60, bf16[1,2,512,2048]{3,2,1,0:T(8,128)(2,1)} %param.10), kind=kOutput, calls=%fused_computation.10 | convolution fusion | flops 134283264 | bytes 2752512 | tf_op jit(solution)/shard_map/dot_general | solution.py:54
  (13 shorter events, 0.2 us)
Async XLA Ops:
  0.0 54.6 %copy-start = (bf16[512,64]{0,1:T(8,128)(2,1)S(1)}, bf16[512,64]{0,1:T(8,128)(2,1)}, u32[]{:S(2)}) copy-start(bf16[512,64]{0,1:T(8,128)(2,1)} %param.16) | copy-start | bytes 196612
  1.0 31.6 %collective-permute-start = (bf16[512,64]{0,1:T(8,128)(2,1)S(1)}, bf16[512,64]{0,1:T(8,128)(2,1)S(1)}, u32[]{:S(2)}, u32[]{:S(2)}) collective-permute-start(bf16[512,64]{0,1:T(8,128)(2,1)S(1)} %convert_element_type.10), channel_id=1, source_target_pairs={{0,1},{1,2},{2,3},{3,0},{4,5},{5,6},{6,7},{7,4},{8,9},{9,10},{10,1... | collective-permute-start | bytes 196616 | tf_op jit(solution)/shard_map/ppermute | solution.py:44
  1.5 32.5 %collective-permute-start.2 = (bf16[512,64]{0,1:T(8,128)(2,1)S(1)}, bf16[512,64]{0,1:T(8,128)(2,1)S(1)}, u32[]{:S(2)}, u32[]{:S(2)}) collective-permute-start(bf16[512,64]{0,1:T(8,128)(2,1)S(1)} %convert_element_type.10), channel_id=1, source_target_pairs={{1,0},{2,1},{3,2},{0,3},{5,4},{6,5},{7,6},{4,7},{9,8},{10,9},{11,1... | collective-permute-start | bytes 196616 | tf_op jit(solution)/shard_map/ppermute | solution.py:46
  32.6 3.7 %collective-permute-start.1 = (bf16[512,64]{0,1:T(8,128)(2,1)S(1)}, bf16[512,64]{0,1:T(8,128)(2,1)S(1)}, u32[]{:S(2)}, u32[]{:S(2)}) collective-permute-start(bf16[512,64]{0,1:T(8,128)(2,1)S(1)} %collective-permute-done), channel_id=1, source_target_pairs={{0,1},{1,2},{2,3},{3,0},{4,5},{5,6},{6,7},{7,4},{8,9},{9,10},{10,1... | collective-permute-start | bytes 196616 | tf_op jit(solution)/shard_map/ppermute | solution.py:44
  36.9 17.8 %collective-permute-start.6 = (bf16[2048,64]{0,1:T(8,128)(2,1)S(1)}, bf16[2048,64]{0,1:T(8,128)(2,1)S(1)}, u32[]{:S(2)}, u32[]{:S(2)}) collective-permute-start(bf16[2048,64]{0,1:T(8,128)(2,1)S(1)} %bitcast.56), channel_id=1, source_target_pairs={{8,0},{12,4},{9,1},{13,5},{10,2},{14,6},{11,3},{15,7},{24,16},{28,... | collective-permute-start | bytes 786440 | tf_op jit(solution)/shard_map/ppermute | solution.py:16
  38.2 16.5 %collective-permute-start.3 = (bf16[2048,64]{0,1:T(8,128)(2,1)S(1)}, bf16[2048,64]{0,1:T(8,128)(2,1)S(1)}, u32[]{:S(2)}, u32[]{:S(2)}) collective-permute-start(bf16[2048,64]{0,1:T(8,128)(2,1)S(1)} %bitcast.57), channel_id=1, source_target_pairs={{0,8},{4,12},{1,9},{5,13},{2,10},{6,14},{3,11},{7,15},{16,24},{20,... | collective-permute-start | bytes 786440 | tf_op jit(solution)/shard_map/ppermute | solution.py:16
  43.7 11.0 %collective-permute-start.4 = (bf16[2048,64]{0,1:T(8,128)(2,1)S(1)}, bf16[2048,64]{0,1:T(8,128)(2,1)S(1)}, u32[]{:S(2)}, u32[]{:S(2)}) collective-permute-start(bf16[2048,64]{0,1:T(8,128)(2,1)S(1)} %bitcast.58), channel_id=1, source_target_pairs={{0,4},{4,8},{8,12},{1,5},{5,9},{9,13},{2,6},{6,10},{10,14},{3,7},{... | collective-permute-start | bytes 786440 | tf_op jit(solution)/shard_map/ppermute | solution.py:16
  47.3 11.3 %collective-permute-start.5 = (bf16[2048,64]{0,1:T(8,128)(2,1)S(1)}, bf16[2048,64]{0,1:T(8,128)(2,1)S(1)}, u32[]{:S(2)}, u32[]{:S(2)}) collective-permute-start(bf16[2048,64]{0,1:T(8,128)(2,1)S(1)} %bitcast.59), channel_id=1, source_target_pairs={{4,0},{8,4},{12,8},{5,1},{9,5},{13,9},{6,2},{10,6},{14,10},{7,3},{... | collective-permute-start | bytes 786440 | tf_op jit(solution)/shard_map/ppermute | solution.py:16
